TPU v7x, 32 devices: a whole 2x2x4 slice. The times are simulated.
32 devices in a mesh: batch: 4 (over x, core), neuron: 8 (over z, y).
Axes of the slice: x: 2, y: 2, z: 4, core: 2. Of those that a mesh axis runs over, the one named last changes fastest.
Arguments:
- tokens: bfloat16 [2, 256, 12288], P(None, 'neuron', 'batch'), may hold values from -6 to 6
- ln_gain: float32 [12288], P('batch'), may hold values from 0.25 to 1.75
- ln_bias: float32 [12288], P('batch'), may hold values from -3 to 3
- up_weight: bfloat16 [12288, 24576], P('batch', 'neuron'), may hold values from -0.0546875 to 0.0546875
- up_bias: float32 [24576], P('neuron'), may hold values from -3 to 3
- down_weight: bfloat16 [24576, 12288], P('neuron', 'batch'), may hold values from -0.078125 to 0.078125
- down_bias: float32 [12288], P('batch'), may hold values from -3 to 3
- active: int32 [2, 2, 48], replicated, may hold values from 0 to 191, all different within a row
Outputs:
- mixed: bfloat16 [2, 256, 12288], P(None, 'neuron', 'batch')
Inputs may be any that keep to these rules, and one draw needn't show every extreme that they name: `active`: each row block of each; despite its name it splits features, not a batch step lists 48 distinct neuron block numbers; every number appears in some list.
All inputs are finite; a program needn't handle non-finite values.
Results may differ from a plain program's by a relative error of at most 0.0044.
Values may be sent and summed in bfloat16 or wider, within the bound.
No kernel may reach another device: no remote copies, remote signals or barrier semaphores. Data moves between devices by JAX's collectives and lax.ppermute only.
A program may use at most 128 MiB of HBM per device.

v0:
```python
import jax
import jax.numpy as jnp
from jax import lax
from jax.sharding import PartitionSpec as P

D = 12288
BLK = 128
RB = 128
STEPS = 2


epsilon = 1e-05


def local_table(listed, first_block, local_blocks):
    block_ids = first_block + jnp.arange(local_blocks, dtype=jnp.int32)
    return jnp.any(listed[:, :, None] == block_ids[None, None, :], axis=1).astype(jnp.float32)


def activate(preact, up_bias, table, first_row):
    row_total = preact.shape[0]
    local_blocks = table.shape[1]
    row_blocks = (first_row + jnp.arange(row_total, dtype=jnp.int32)) // RB
    block_count = table.shape[0]
    onehot = (row_blocks[:, None] == jnp.arange(block_count, dtype=jnp.int32)[None, :]).astype(
        jnp.float32
    )
    row_mask = jnp.dot(onehot, table, preferred_element_type=jnp.float32)
    shaped = jnp.maximum(preact + up_bias, 0.0).reshape(row_total, local_blocks, BLK)
    return (
        (shaped * row_mask[:, :, None]).reshape(row_total, local_blocks * BLK).astype(jnp.bfloat16)
    )


def normalize(inputs, sum_total, square_total, ln_gain, ln_bias):
    average = sum_total / D
    spread = square_total / D - average * average
    scaled = (inputs - average[:, None]) * lax.rsqrt(spread + epsilon)[:, None]
    return (scaled * ln_gain + ln_bias).astype(jnp.bfloat16)


def local(tokens, ln_gain, ln_bias, up_weight, up_bias, down_weight, down_bias, active):
    local_rows = tokens.shape[1]
    local_neurons = up_weight.shape[1]
    local_blocks = local_neurons // BLK
    neuron_index = lax.axis_index("neuron")
    batch_index = lax.axis_index("batch")
    all_rows = local_rows * lax.axis_size("neuron")
    share_rows = all_rows // lax.axis_size("batch")
    first_block = neuron_index * local_blocks
    results = []
    for step_index in range(STEPS):
        residual = tokens[step_index]
        residual_wide = residual.astype(jnp.float32)
        table = local_table(active[step_index], first_block, local_blocks)
        sum_total, square_total = lax.psum(
            (jnp.sum(residual_wide, axis=-1), jnp.sum(residual_wide * residual_wide, axis=-1)),
            "batch",
        )
        normed = normalize(residual_wide, sum_total, square_total, ln_gain, ln_bias)
        gathered = lax.all_gather(normed, "neuron", axis=0, tiled=True)
        preact = lax.psum_scatter(
            jnp.dot(gathered, up_weight, preferred_element_type=jnp.float32),
            "batch",
            scatter_dimension=0,
            tiled=True,
        )
        hidden_share = activate(preact, up_bias, table, batch_index * share_rows)
        hidden_all = lax.all_gather(hidden_share, "batch", axis=0, tiled=True)
        projected = lax.psum_scatter(
            jnp.dot(hidden_all, down_weight, preferred_element_type=jnp.float32),
            "neuron",
            scatter_dimension=0,
            tiled=True,
        )
        results.append((projected + residual_wide + down_bias).astype(jnp.bfloat16))
    return jnp.stack(results)


def solution(mesh):
    in_specs = (
        P(None, "neuron", "batch"),
        P("batch"),
        P("batch"),
        P("batch", "neuron"),
        P("neuron"),
        P("neuron", "batch"),
        P("batch"),
        P(),
    )
    out_specs = P(None, "neuron", "batch")
    return jax.shard_map(local, mesh=mesh, in_specs=in_specs, out_specs=out_specs, check_vma=False)
```

profile of v0, /device:TPU:0, one launch (start us, length us, event | category | flops | bytes accessed | tf_op | source)
XLA Modules:
  0.0 396.0 jit_solution(18306868682773329891)
XLA Ops:
  6.5 0.0 all-gather.5.cloned.1.call-start
  6.5 1.2 convert_reduce_fusion.1
  7.7 1.2 fusion.12
  8.9 8.4 %all-reduce = (f32[32]{0:T(128)S(1)}, f32[32]{0:T(128)S(1)}, f32[32]{0:T(128)S(1)}, f32[32]{0:T(128)S(1)}) all-reduce(f32[32]{0:T(128)S(1)} %get-tuple-element.8, f32[32]{0:T(128)S(1)} %get-tuple-element.6, f32[32]{0:T(128)S(1)} %get-tuple-element.7, f32[32]{0:T(128)S(1)} %get-tuple-element.5), channel_id=1, replica_groups=mesh['batch'=4,'neuron'=8] {'batch'}, use_global_device_ids=true, to_apply=%region_10.11 | all-reduce | flops 128 | bytes 1024 | tf_op jit(solution)/shard_map/psum | solution.py:56
  17.3 2.0 fusion.11
  19.3 0.0 all-gather.5.cloned.1.call-update
  19.3 0.0 all-gather.9.cloned.1.call-start
  19.4 0.7 all-gather.9.cloned.1.call-update
  20.1 0.0 reduce-scatter.5.cloned.1.call-start
  20.1 43.9 %all-gather.5.cloned.1.call-done = bf16[256,3072]{1,0:T(8,128)(2,1)} async-done(((bf16[32,3072]{1,0:T(8,128)(2,1)}), bf16[256,3072]{1,0:T(8,128)(2,1)}) %all-gather.5.cloned.1.call-update) | async-done | bytes 1572880 | tf_op jit(solution)/shard_map/all_gather | solution.py:61
  64.0 10.6 %fusion.28 = f32[256,3072]{1,0:T(8,128)} fusion(bf16[256,3072]{1,0:T(8,128)(2,1)} %all-gather.5.cloned.1.call-done, bf16[3072,3072]{1,0:T(8,128)(2,1)} %param.11), kind=kOutput, calls=%fused_computation.49 | convolution fusion | flops 4831838208 | bytes 23592960 | tf_op jit(solution)/shard_map/dot_general | solution.py:63
  74.6 0.0 reduce-scatter.5.cloned.1.call-update
  74.6 0.0 reduce-scatter.9.cloned.1.call-start
  74.6 34.2 %all-gather.9.cloned.1.call-done = bf16[256,3072]{1,0:T(8,128)(2,1)} async-done(((bf16[32,3072]{1,0:T(8,128)(2,1)}), bf16[256,3072]{1,0:T(8,128)(2,1)}) %all-gather.9.cloned.1.call-update) | async-done | bytes 1572880 | tf_op jit(solution)/shard_map/all_gather | solution.py:61
  108.8 11.1 %fusion.30 = f32[256,3072]{1,0:T(8,128)} fusion(bf16[256,3072]{1,0:T(8,128)(2,1)} %all-gather.9.cloned.1.call-done, bf16[3072,3072]{1,0:T(8,128)(2,1)} %param.11), kind=kOutput, calls=%fused_computation.51 | convolution fusion | flops 4831838208 | bytes 23592960 | tf_op jit(solution)/shard_map/dot_general | solution.py:63
  119.9 0.0 copy-start.3
  119.9 0.0 copy-start.1
  119.9 0.0 reduce-scatter.9.cloned.1.call-update
  119.9 0.0 all-gather.11.cloned.1.call-start
  120.0 0.6 copy-done.3
  120.6 0.2 compare_reduce_fusion.1
  120.8 0.2 fusion.24
  121.0 0.2 fusion.25
  121.2 26.4 %reduce-scatter.5.cloned.1.call-done = f32[64,3072]{1,0:T(8,128)} async-done(((f32[256,3072]{1,0:T(8,128)}), f32[64,3072]{1,0:T(8,128)}) %reduce-scatter.5.cloned.1.call-update) | async-done | bytes 786448 | tf_op jit(solution)/shard_map/reduce_scatter | solution.py:62
  147.6 40.3 %reduce-scatter.9.cloned.1.call-done = f32[64,3072]{1,0:T(8,128)} async-done(((f32[256,3072]{1,0:T(8,128)}), f32[64,3072]{1,0:T(8,128)}) %reduce-scatter.9.cloned.1.call-update) | async-done | bytes 786448 | tf_op jit(solution)/shard_map/reduce_scatter | solution.py:62
  187.9 0.3 mul.87
  188.2 0.3 mul.79
  188.5 0.0 copy-done.1
  188.5 2.7 fusion.1
  191.2 0.0 all-gather.11.cloned.1.call-update
  191.2 0.0 all-gather.7.cloned.1.call-start
  191.2 0.5 all-gather.7.cloned.1.call-update
  191.8 0.0 reduce-scatter.11.cloned.1.call-start
  191.8 19.2 %all-gather.11.cloned.1.call-done = bf16[256,3072]{1,0:T(8,128)(2,1)} async-done(((bf16[64,3072]{1,0:T(8,128)(2,1)}), bf16[256,3072]{1,0:T(8,128)(2,1)}) %all-gather.11.cloned.1.call-update) | async-done | bytes 1572880 | tf_op jit(solution)/shard_map/all_gather | solution.py:69
  211.0 10.6 %fusion.31 = f32[256,3072]{1,0:T(8,128)} fusion(bf16[256,3072]{1,0:T(8,128)(2,1)} %all-gather.11.cloned.1.call-done, bf16[3072,3072]{1,0:T(8,128)(2,1)} %param.13), kind=kOutput, calls=%fused_computation.52 | convolution fusion | flops 4831838208 | bytes 23592960 | tf_op jit(solution)/shard_map/dot_general | solution.py:71
  221.5 0.0 reduce-scatter.11.cloned.1.call-update
  221.6 0.0 reduce-scatter.7.cloned.1.call-start
  221.6 10.4 %all-gather.7.cloned.1.call-done = bf16[256,3072]{1,0:T(8,128)(2,1)} async-done(((bf16[64,3072]{1,0:T(8,128)(2,1)}), bf16[256,3072]{1,0:T(8,128)(2,1)}) %all-gather.7.cloned.1.call-update) | async-done | bytes 1572880 | tf_op jit(solution)/shard_map/all_gather | solution.py:69
  232.1 10.6 %fusion.29 = f32[256,3072]{1,0:T(8,128)} fusion(bf16[256,3072]{1,0:T(8,128)(2,1)} %all-gather.7.cloned.1.call-done, bf16[3072,3072]{1,0:T(8,128)(2,1)} %param.13), kind=kOutput, calls=%fused_computation.50 | convolution fusion | flops 4831838208 | bytes 23592960 | tf_op jit(solution)/shard_map/dot_general | solution.py:71
  242.6 0.0 copy-start
  242.6 0.0 reduce-scatter.7.cloned.1.call-update
  242.7 67.5 %reduce-scatter.11.cloned.1.call-done = f32[32,3072]{1,0:T(8,128)} async-done(((f32[256,3072]{1,0:T(8,128)}), f32[32,3072]{1,0:T(8,128)}) %reduce-scatter.11.cloned.1.call-update) | async-done | bytes 393232 | tf_op jit(solution)/shard_map/reduce_scatter | solution.py:70
  310.1 77.1 %reduce-scatter.7.cloned.1.call-done = f32[32,3072]{1,0:T(8,128)} async-done(((f32[256,3072]{1,0:T(8,128)}), f32[32,3072]{1,0:T(8,128)}) %reduce-scatter.7.cloned.1.call-update) | async-done | bytes 393232 | tf_op jit(solution)/shard_map/reduce_scatter | solution.py:70
  387.2 0.0 copy-done
  387.2 0.0 copy-done.2
  387.2 1.2 fusion.23
  388.4 0.0 copy-start.4
  388.4 0.7 copy-done.4
  (6 shorter events, 0.0 us)
Async XLA Ops:
  6.5 57.5 %all-gather.5.cloned.1.call-start = ((), (), s32[]{:S(2)}) async-start(), calls=%async_computation.4 | async-start | bytes 1769472 | tf_op jit(solution)/shard_map/all_gather | solution.py:61
  19.3 89.5 %all-gather.9.cloned.1.call-start = ((), (), s32[]{:S(2)}) async-start(), calls=%async_computation.8 | async-start | bytes 1769472 | tf_op jit(solution)/shard_map/all_gather | solution.py:61
  20.1 127.5 %reduce-scatter.5.cloned.1.call-start = ((), (), s32[]{:S(2)}) async-start(), calls=%async_computation.5 | async-start | bytes 3932160 | tf_op jit(solution)/shard_map/reduce_scatter | solution.py:62
  74.6 113.3 %reduce-scatter.9.cloned.1.call-start = ((), (), s32[]{:S(2)}) async-start(), calls=%async_computation.9 | async-start | bytes 3932160 | tf_op jit(solution)/shard_map/reduce_scatter | solution.py:62
  119.9 0.7 copy-start.3
  119.9 68.6 %copy-start.1 = (f32[3072]{0:T(1024)S(1)}, f32[3072]{0:T(1024)}, u32[]{:S(2)}) copy-start(f32[3072]{0:T(1024)} %param.12) | copy-start | bytes 36868
  119.9 91.1 %all-gather.11.cloned.1.call-start = ((), (), s32[]{:S(2)}) async-start(), calls=%async_computation.10 | async-start | bytes 1966080 | tf_op jit(solution)/shard_map/all_gather | solution.py:69
  191.2 40.9 %all-gather.7.cloned.1.call-start = ((), (), s32[]{:S(2)}) async-start(), calls=%async_computation.6 | async-start | bytes 1966080 | tf_op jit(solution)/shard_map/all_gather | solution.py:69
  191.8 118.4 %reduce-scatter.11.cloned.1.call-start = ((), (), s32[]{:S(2)}) async-start(), calls=%async_computation.11 | async-start | bytes 3538944 | tf_op jit(solution)/shard_map/reduce_scatter | solution.py:70
  221.6 165.6 %reduce-scatter.7.cloned.1.call-start = ((), (), s32[]{:S(2)}) async-start(), calls=%async_computation.7 | async-start | bytes 3538944 | tf_op jit(solution)/shard_map/reduce_scatter | solution.py:70
  242.6 144.6 %copy-start = (bf16[2,32,3072]{2,1,0:T(8,128)(2,1)S(1)}, bf16[2,32,3072]{2,1,0:T(8,128)(2,1)}, u32[]{:S(2)}) copy-start(bf16[2,32,3072]{2,1,0:T(8,128)(2,1)} %param.8) | copy-start | bytes 1179652
  242.6 144.6 %copy-start.2 = (f32[3072]{0:T(1024)S(1)}, f32[3072]{0:T(1024)}, u32[]{:S(2)}) copy-start(f32[3072]{0:T(1024)} %param.14) | copy-start | bytes 36868
  388.4 0.7 copy-start.4
Sparse Core Ops, SparseCore 0:
  19.5 44.4 all-gather.4
  66.2 42.5 all-gather.8
  111.4 36.2 reduce-scatter.4
  150.0 37.8 reduce-scatter.8
  191.3 19.6 all-gather.10
  212.4 19.6 all-gather.6
  235.6 74.4 reduce-scatter.10
  313.7 73.4 reduce-scatter.6
where the time goes:
time: 396 us
  waiting for transfers between devices  320 us (81%)
  matrix products  43.2 us (11%)
  between operations  13.6 us (3%)
  other arithmetic  8.54 us (2%)
  blocking collectives  8.37 us (2%)
    reduce_scatter x2, waiting for transfers between devices, local(): lax.psum_scatter(jnp.dot(hidden_all, down_weight, preferred_element_type=...  145 us
    all_gather x2, waiting for transfers between devices, local(): gathered = lax.all_gather(normed, 'neuron', axis=0, tiled=True)  78 us
    reduce_scatter x2, waiting for transfers between devices, local(): lax.psum_scatter(jnp.dot(gathered, up_weight, preferred_element_type=jnp....  66.7 us
    all_gather x2, waiting for transfers between devices, local(): hidden_all = lax.all_gather(hidden_share, 'batch', axis=0, tiled=True)  29.6 us
    dot_general x2, matrix products, local(): jnp.dot(gathered, up_weight, preferred_element_type=jnp.float32)  21.6 us
    dot_general x2, matrix products, local(): jnp.dot(hidden_all, down_weight, preferred_element_type=jnp.float32)  21.2 us
    psum x1, blocking collectives, local(): lax.psum((jnp.sum(residual_wide, axis=-1), jnp.sum(residual_wide * residu...  8.37 us
  transfers between devices with their start and end apart: 8, of which 8 were waited for; matrix products, arithmetic and copies ran while one was open for 11% of the time, Pallas kernels for 0%

commit v1 on v0

v1 whole, which is shorter than its diff:
```python
import functools

import jax
import jax.numpy as jnp
from jax import lax
from jax.experimental import pallas as pl
from jax.experimental.pallas import tpu as pltpu
from jax.sharding import PartitionSpec as P

BLK = 128
RB = 128
CORES = 2
EPSILON = 1e-05
BUFFERS = 3
F32 = jnp.float32
BF16 = jnp.bfloat16
ANY = pl.BlockSpec(memory_space=pl.ANY)
SMEM = pl.BlockSpec(memory_space=pltpu.SMEM)
VMEM = pl.BlockSpec(memory_space=pltpu.VMEM)


def ring_order(mesh):
    devices = mesh.devices[0] if mesh.axis_names[0] == "batch" else mesh.devices[:, 0]
    count = len(devices)
    points = [tuple(getattr(d, "coords", (0, 0, i))) for i, d in enumerate(devices)]
    axes = [a for a in range(3) if len({p[a] for p in points}) > 1]
    if len(axes) != 2:
        return list(range(count))
    for first, second in (axes, axes[::-1]):
        rows = sorted({p[first] for p in points})
        columns = sorted({p[second] for p in points})
        if len(rows) % 2 == 0:
            break
    at = {(p[first], p[second]): i for i, p in enumerate(points)}
    walk = []
    for position, row in enumerate(rows):
        inner = columns if position == 0 else columns[1:]
        walk += [(row, column) for column in (inner if position % 2 == 0 else inner[::-1])]
    walk += [(row, columns[0]) for row in rows[:0:-1]]
    return [at[point] for point in walk]


def table_kernel(lists, picks, limit, first_ref, active_ref, block_ref, item_ref, count_ref):
    first = first_ref[0]

    def per_list(index, carry):
        slot, item = carry

        def per_pick(pick, slot):
            block = active_ref[index * picks + pick] - first
            block_ref[slot] = block
            return slot + jnp.where((block >= 0) & (block < limit[0]), 1, 0)

        end = lax.fori_loop(0, picks, per_pick, slot)

        def per_pair(pair, item):
            left = slot + 2 * pair
            item_ref[0, item] = index
            item_ref[1, item] = left
            item_ref[2, item] = jnp.where(left + 1 < end, left + 1, limit[1])
            return item + 1

        item = lax.fori_loop(0, (end - slot + 1) // 2, per_pair, item)
        return end, item

    slot, item = lax.fori_loop(0, lists, per_list, (0, 0))
    count_ref[0] = item
    count_ref[1] = slot


def make_tables(active, first_block, local_blocks, capacity):
    steps, row_blocks, picks = active.shape
    lists = steps * row_blocks
    return pl.pallas_call(
        functools.partial(table_kernel, lists, picks, (local_blocks, capacity)),
        out_shape=(
            jax.ShapeDtypeStruct((capacity + 1,), jnp.int32),
            jax.ShapeDtypeStruct((3, capacity + lists), jnp.int32),
            jax.ShapeDtypeStruct((2,), jnp.int32),
        ),
        in_specs=[SMEM, SMEM],
        out_specs=(SMEM, SMEM, SMEM),
        name="tables",
    )(first_block.reshape(1), active.reshape(-1))


def up_kernel(pieces_count, row_blocks, half, *refs):
    place_ref, core_ref, block_ref, item_ref, count_ref, weight_ref = refs[:6]
    pieces = refs[6 : 6 + pieces_count]
    keep_ref, send_ref, rows_ref, weights, total, row_sem, weight_sem = refs[6 + pieces_count :]
    shards = RB // rows_ref.shape[2]
    items = count_ref[0]

    def weight_copies(item):
        buffer = lax.rem(item, BUFFERS)
        left = item_ref[1, item]
        right = item_ref[2, item]
        right = jnp.where(right < 2 * half, right, left)
        return [
            pltpu.make_async_copy(
                weight_ref.at[:, pl.ds(pl.multiple_of(block_ref[slot] * BLK, BLK), BLK)],
                weights.at[buffer, :, pl.ds(side * BLK, BLK)],
                weight_sem.at[buffer, side],
            )
            for side, slot in enumerate((left, right))
        ]

    row_copies = [
        pltpu.make_async_copy(piece, rows_ref.at[index], row_sem.at[index])
        for index, piece in enumerate(pieces)
    ]
    for copy in row_copies:
        copy.start()
    for ahead in range(BUFFERS - 1):

        @pl.when(ahead < items)
        def _():
            for copy in weight_copies(ahead):
                copy.start()

    for copy in row_copies:
        copy.wait()

    def per_item(item, carry):
        @pl.when(item + BUFFERS - 1 < items)
        def _():
            for copy in weight_copies(item + BUFFERS - 1):
                copy.start()

        for copy in weight_copies(item):
            copy.wait()
        index = item_ref[0, item]
        step = index // row_blocks
        first = (index - step * row_blocks) * shards
        rows = jnp.concatenate(
            [rows_ref[place_ref[first + shard], step] for shard in range(shards)], axis=0
        )
        result = jnp.dot(rows, weights[lax.rem(item, BUFFERS)], preferred_element_type=F32)
        total[item_ref[1, item]] = result[:, :BLK]
        total[item_ref[2, item]] = result[:, BLK:]
        return carry

    lax.fori_loop(0, items, per_item, 0)
    mine = core_ref[0] * half
    keep_ref[...] = total[pl.ds(mine, half)]
    send_ref[...] = total[pl.ds(half - mine, half)].astype(BF16)


def up_project(place, core, tables, weight, pieces, row_blocks, capacity):
    half = capacity // CORES
    steps, shard_rows, width = pieces[0].shape
    return pl.pallas_call(
        functools.partial(up_kernel, len(pieces), row_blocks, half),
        out_shape=(
            jax.ShapeDtypeStruct((half, RB, BLK), F32),
            jax.ShapeDtypeStruct((half, RB, BLK), BF16),
        ),
        in_specs=[SMEM] * 5 + [ANY] * (1 + len(pieces)),
        out_specs=(VMEM, VMEM),
        scratch_shapes=[
            pltpu.VMEM((len(pieces), steps, shard_rows, width), BF16),
            pltpu.VMEM((BUFFERS, width, 2 * BLK), BF16),
            pltpu.VMEM((capacity + 1, RB, BLK), F32),
            pltpu.SemaphoreType.DMA((len(pieces),)),
            pltpu.SemaphoreType.DMA((BUFFERS, 2)),
        ],
        compiler_params=pltpu.CompilerParams(vmem_limit_bytes=40 << 20),
        cost_estimate=pl.CostEstimate(
            flops=2 * capacity * RB * BLK * width,
            bytes_accessed=capacity * BLK * width * 2,
            transcendentals=0,
        ),
        name="up",
    )(place, core, *tables, weight, *pieces)


def down_kernel(row_blocks, half, *refs):
    place_ref, core_ref, block_ref, item_ref, count_ref, weight_ref, own_ref, other_ref = refs[:8]
    far_ref, chain_ref, give_ref, home_ref = refs[8:12]
    hidden, weights, total, parts, hidden_sem, weight_sem, out_sem = refs[12:]
    shard_rows = parts.shape[2]
    shards = RB // shard_rows
    width = parts.shape[3]
    items = count_ref[0]
    mine = core_ref[0] * half

    def weight_copies(item):
        buffer = lax.rem(item, BUFFERS)
        left = item_ref[1, item]
        right = item_ref[2, item]
        right = jnp.where(right < 2 * half, right, left)
        return [
            pltpu.make_async_copy(
                weight_ref.at[pl.ds(pl.multiple_of(block_ref[slot] * BLK, BLK), BLK), :],
                weights.at[buffer, pl.ds(side * BLK, BLK), :],
                weight_sem.at[buffer, side],
            )
            for side, slot in enumerate((left, right))
        ]

    hidden_copies = [
        pltpu.make_async_copy(own_ref, hidden.at[pl.ds(mine, half)], hidden_sem.at[0]),
        pltpu.make_async_copy(other_ref, hidden.at[pl.ds(half - mine, half)], hidden_sem.at[1]),
    ]
    for copy in hidden_copies:
        copy.start()
    for ahead in range(BUFFERS - 1):

        @pl.when(ahead < items)
        def _():
            for copy in weight_copies(ahead):
                copy.start()

    hidden[2 * half] = jnp.zeros((RB, BLK), BF16)
    parts[...] = jnp.zeros(parts.shape, BF16)
    for copy in hidden_copies:
        copy.wait()

    def per_item(item, carry):
        @pl.when(item + BUFFERS - 1 < items)
        def _():
            for copy in weight_copies(item + BUFFERS - 1):
                copy.start()

        for copy in weight_copies(item):
            copy.wait()
        index = item_ref[0, item]
        before = item_ref[0, jnp.maximum(item - 1, 0)]
        after = item_ref[0, jnp.minimum(item + 1, items - 1)]
        opens = (item == 0) | (before != index)
        closes = (item == items - 1) | (after != index)
        values = jnp.concatenate([hidden[item_ref[1, item]], hidden[item_ref[2, item]]], axis=1)
        buffer = lax.rem(item, BUFFERS)
        piece = 512 if width % 512 == 0 else BLK

        @pl.when(opens)
        def _():
            for start in range(0, width, piece):
                total[:, start : start + piece] = jnp.dot(
                    values,
                    weights[buffer, :, start : start + piece],
                    preferred_element_type=F32,
                )

        @pl.when(jnp.logical_not(opens))
        def _():
            for start in range(0, width, piece):
                total[:, start : start + piece] += jnp.dot(
                    values,
                    weights[buffer, :, start : start + piece],
                    preferred_element_type=F32,
                )

        @pl.when(closes)
        def _():
            step = index // row_blocks
            first = (index - step * row_blocks) * shards
            for shard in range(shards):
                parts[place_ref[first + shard], step] = total[
                    shard * shard_rows : (shard + 1) * shard_rows
                ].astype(BF16)

        return carry

    lax.fori_loop(0, items, per_item, 0)
    count = chain_ref.shape[0]
    outs = [
        pltpu.make_async_copy(parts.at[0], home_ref, out_sem.at[0]),
        pltpu.make_async_copy(parts.at[2 * count + 1], far_ref, out_sem.at[1]),
    ]
    for k in range(1, count + 1):
        outs.append(
            pltpu.make_async_copy(parts.at[2 * k], chain_ref.at[k - 1], out_sem.at[2 * k])
        )
        outs.append(
            pltpu.make_async_copy(parts.at[2 * k - 1], give_ref.at[k - 1], out_sem.at[2 * k + 1])
        )
    for copy in outs:
        copy.start()
    for copy in outs:
        copy.wait()


def down_project(place, core, tables, weight, own, other, shape, ring, row_blocks, capacity):
    half = capacity // CORES
    steps, shard_rows, width = shape
    count = ring // 2 - 1
    return pl.pallas_call(
        functools.partial(down_kernel, row_blocks, half),
        out_shape=(
            jax.ShapeDtypeStruct(shape, BF16),
            jax.ShapeDtypeStruct((count,) + shape, BF16),
            jax.ShapeDtypeStruct((count,) + shape, BF16),
            jax.ShapeDtypeStruct(shape, BF16),
        ),
        in_specs=[SMEM] * 5 + [ANY] * 3,
        out_specs=(ANY,) * 4,
        scratch_shapes=[
            pltpu.VMEM((capacity + 1, RB, BLK), BF16),
            pltpu.VMEM((BUFFERS, 2 * BLK, width), BF16),
            pltpu.VMEM((RB, width), F32),
            pltpu.VMEM((ring,) + shape, BF16),
            pltpu.SemaphoreType.DMA((2,)),
            pltpu.SemaphoreType.DMA((BUFFERS, 2)),
            pltpu.SemaphoreType.DMA((ring,)),
        ],
        compiler_params=pltpu.CompilerParams(vmem_limit_bytes=40 << 20),
        cost_estimate=pl.CostEstimate(
            flops=2 * capacity * RB * BLK * width,
            bytes_accessed=capacity * BLK * width * 2,
            transcendentals=0,
        ),
        name="down",
    )(place, core, *tables, weight, own, other)


def solution(mesh):
    batch = mesh.shape["batch"]
    ring = mesh.shape["neuron"]
    order = ring_order(mesh)
    position_of = [order.index(n) for n in range(ring)]
    pair = [(b, b ^ 1) for b in range(batch)]
    chips = batch // CORES
    hop = [
        (b * ring + order[p], b * ring + order[(p + (1 if b % CORES == 0 else -1)) % ring])
        for b in range(batch)
        for p in range(ring)
    ]

    def to_partner(value):
        return lax.ppermute(value, "batch", pair)

    def onward(value):
        return lax.ppermute(value, ("batch", "neuron"), hop)

    def over_chips(value):
        return [
            lax.ppermute(
                value,
                "batch",
                [
                    (x * CORES + c, (x + d) % chips * CORES + c)
                    for x in range(chips)
                    for c in range(CORES)
                ],
            )
            for d in range(1, chips)
        ]

    def local(tokens, ln_gain, ln_bias, up_weight, up_bias, down_weight, down_bias, active):
        steps, shard_rows, width = tokens.shape
        _, row_blocks, picks = active.shape
        lists = steps * row_blocks
        local_blocks = up_weight.shape[1] // BLK
        all_blocks = local_blocks * ring
        capacity = min(local_blocks * lists, lists * picks - (all_blocks - local_blocks))
        capacity += capacity % CORES
        half = capacity // CORES
        model = width * batch
        far = ring // 2

        neuron_index = lax.axis_index("neuron")
        core = lax.axis_index("batch") % CORES
        here = jnp.array(position_of, jnp.int32)[neuron_index]
        away = (jnp.array(position_of, jnp.int32) - here) % ring
        away = jnp.where(core == 0, (ring - away) % ring, away)
        place = jnp.where(
            away == 0,
            0,
            jnp.where(
                away < far, 2 * away - 1, jnp.where(away == far, ring - 1, 2 * (ring - away))
            ),
        ).astype(jnp.int32)
        core = core.astype(jnp.int32).reshape(1)
        tables = make_tables(
            active, (neuron_index * local_blocks).astype(jnp.int32), local_blocks, capacity
        )

        wide = tokens.astype(F32)
        sums = jnp.stack([jnp.sum(wide, axis=-1), jnp.sum(wide * wide, axis=-1)])
        sums = sums + to_partner(sums)
        sums = sum(over_chips(sums), sums)
        average = sums[0] / model
        spread = sums[1] / model - average * average
        normed = (
            (wide - average[..., None]) * lax.rsqrt(spread + EPSILON)[..., None] * ln_gain
            + ln_bias
        ).astype(BF16)

        partner = to_partner(normed)
        gathered = [[] for _ in range(ring)]
        for step in range(steps):
            gathered[0].append(normed[step])
            message = jnp.stack([normed[step], partner[step]])
            for k in range(1, far):
                message = onward(message)
                gathered[2 * k - 1].append(message[0])
                gathered[2 * k].append(to_partner(message[1]))
            gathered[ring - 1].append(onward(message[0]))
        pieces = [jnp.stack(piece) for piece in gathered]

        keep, send = up_project(place, core, tables, up_weight, pieces, row_blocks, capacity)
        chip_sum = keep + to_partner(send).astype(F32)
        preact = sum((v.astype(F32) for v in over_chips(chip_sum.astype(BF16))), chip_sum)
        slots = lax.dynamic_slice_in_dim(tables[0], core[0] * half, half)
        bias = up_bias.reshape(local_blocks, BLK)[slots]
        hidden = jnp.maximum(preact + bias[:, None, :], 0.0).astype(BF16)
        hidden_other = to_partner(hidden)

        far_part, chain, give, home = down_project(
            place,
            core,
            tables,
            down_weight,
            hidden,
            hidden_other,
            tokens.shape,
            ring,
            row_blocks,
            capacity,
        )
        taken = to_partner(give)
        results = []
        for step in range(steps):
            moving = onward(far_part[step])
            for k in range(far - 1, 0, -1):
                mine = chain[k - 1, step].astype(F32)
                others = taken[k - 1, step].astype(F32)
                if k == far - 1:
                    message = jnp.stack([moving.astype(F32) + mine, others])
                else:
                    message = moving.astype(F32) + jnp.stack([mine, others])
                moving = onward(message.astype(BF16))
            rest = to_partner(moving[1])
            results.append(
                (
                    home[step].astype(F32)
                    + moving[0].astype(F32)
                    + rest.astype(F32)
                    + wide[step]
                    + down_bias
                ).astype(BF16)
            )
        return jnp.stack(results)

    in_specs = (
        P(None, "neuron", "batch"),
        P("batch"),
        P("batch"),
        P("batch", "neuron"),
        P("neuron"),
        P("neuron", "batch"),
        P("batch"),
        P(),
    )
    out_specs = P(None, "neuron", "batch")
    return jax.shard_map(local, mesh=mesh, in_specs=in_specs, out_specs=out_specs, check_vma=False)
```

time: 396 us -> 135 us (0.34)
  waiting for transfers between devices: 320 us -> 67.6 us
  matrix products: 43.2 us -> 0 us
  starting transfers between devices: 0.29 us -> 32.9 us
  Pallas kernels: 0 us -> 25.9 us
  between operations: 13.6 us -> 0.42 us
  blocking collectives: 8.37 us -> 0 us
    reduce_scatter x4 -> x0, waiting for transfers between devices: 211 us -> none  [the longest x2 145 us: local(): lax.psum_scatter(jnp.dot(hidden_all, down_weight, preferred_element_type=...]
    all_gather x4 -> x0, waiting for transfers between devices: 108 us -> none  [the longest x2 78 us: local(): gathered = lax.all_gather(normed, 'neuron', axis=0, tiled=True)]
    ppermute x0 -> x31, waiting for transfers between devices: none -> 67.6 us  [the longest x16 49.7 us: onward(): return lax.ppermute(value, ('batch', 'neuron'), hop)]
    dot_general x6 -> x0, matrix products: 43.2 us -> none  [the longest x2 21.6 us: local(): jnp.dot(gathered, up_weight, preferred_element_type=jnp.float32)]
    ppermute x0 -> x31, starting transfers between devices: none -> 32.9 us  [the longest x16 27 us: onward(): return lax.ppermute(value, ('batch', 'neuron'), hop)]
    pallas_call x0 -> x3, Pallas kernels: none -> 25.9 us  [the longest x1 11.5 us: down_project(): pl.pallas_call(functools.partial(down_kernel, row_blocks, half), out_shap...]
    psum x1 -> x0, blocking collectives: 8.37 us -> none  [local(): lax.psum((jnp.sum(residual_wide, axis=-1), jnp.sum(residual_wide * residu...]
  transfers between devices with their start and end apart: 8 -> 31, of which waited for: 8 -> 22; matrix products, arithmetic and copies ran while one was open for 11% -> 3% of each run, Pallas kernels for 0% -> 2%
where the time goes in v1:
time: 135 us
  waiting for transfers between devices  67.6 us (50%)
  starting transfers between devices  32.9 us (24%)
  Pallas kernels  25.9 us (19%)
  other arithmetic  5.41 us (4%)
  local copies, waits for them, and re-layouts  2.27 us (2%)
    ppermute x16, waiting for transfers between devices, onward(): return lax.ppermute(value, ('batch', 'neuron'), hop)  49.7 us
    ppermute x16, starting transfers between devices, onward(): return lax.ppermute(value, ('batch', 'neuron'), hop)  27 us
    pallas_call x1, Pallas kernels, down_project(): pl.pallas_call(functools.partial(down_kernel, row_blocks, half), out_shap...  11.5 us
    pallas_call x1, Pallas kernels, up_project(): pl.pallas_call(functools.partial(up_kernel, len(pieces), row_blocks, half...  11 us
    ppermute x2, waiting for transfers between devices, over_chips(): lax.ppermute(value, 'batch', [(x * CORES + c, (x + d) % chips * CORES + c...  10.6 us
    ppermute x13, waiting for transfers between devices, to_partner(): return lax.ppermute(value, 'batch', pair)  7.28 us
    ppermute x2, starting transfers between devices, over_chips(): lax.ppermute(value, 'batch', [(x * CORES + c, (x + d) % chips * CORES + c...  4.38 us
    pallas_call x1, Pallas kernels, make_tables(): pl.pallas_call(functools.partial(table_kernel, lists, picks, (local_block...  3.36 us
  transfers between devices with their start and end apart: 31, of which 22 were waited for; matrix products, arithmetic and copies ran while one was open for 3% of the time, Pallas kernels for 2%

profile of v1, /device:TPU:0, one launch (start us, length us, event | category | flops | bytes accessed | tf_op | source)
XLA Modules:
  0.0 134.6 jit_solution(6723784108124057062)
XLA Ops:
  0.0 1.2 convert_reduce_fusion
  1.8 0.8 collective-permute-done
  2.6 2.8 %collective-permute-start.1 = (f32[2,2,32]{2,1,0:T(2,128)S(1)}, f32[2,2,32]{2,1,0:T(2,128)S(1)}, u32[]{:S(2)}, u32[]{:S(2)}) collective-permute-start(f32[2,2,32]{2,1,0:T(2,128)S(1)} %fusion.20), channel_id=1, source_target_pairs={{0,16},{8,24},{16,0},{24,8},{1,17},{9,25},{17,1},{25,9},{2,18},{10... | collective-permute-start | bytes 1544 | tf_op jit(solution)/shard_map/ppermute | solution.py:338
  5.4 1.6 %collective-permute-done.1 = f32[2,2,32]{2,1,0:T(2,128)S(1)} collective-permute-done((f32[2,2,32]{2,1,0:T(2,128)S(1)}, f32[2,2,32]{2,1,0:T(2,128)S(1)}, u32[]{:S(2)}, u32[]{:S(2)}) %collective-permute-start.1) | collective-permute-done | bytes 544 | tf_op jit(solution)/shard_map/ppermute | solution.py:338
  7.0 1.2 add_convert_fusion.4.refs_6_
  8.4 1.7 %collective-permute-done.2 = bf16[2,32,3072]{2,1,0:T(8,128)(2,1)S(1)} collective-permute-done((bf16[2,32,3072]{2,1,0:T(8,128)(2,1)S(1)}, bf16[2,32,3072]{2,1,0:T(8,128)(2,1)S(1)}, u32[]{:S(2)}, u32[]{:S(2)}) %collective-permute-start.2) | collective-permute-done | bytes 393248 | tf_op jit(solution)/shard_map/ppermute | solution.py:331
  10.1 2.2 %collective-permute-start.4 = (bf16[2,32,3072]{2,1,0:T(8,128)(2,1)S(1)}, bf16[2,32,3072]{2,1,0:T(8,128)(2,1)S(1)}, u32[]{:S(2)}, u32[]{:S(2)}) collective-permute-start(bf16[2,32,3072]{2,1,0:T(8,128)(2,1)S(1)} %pad_maximum_fusion.1), channel_id=1, source_target_pairs={{0,2},{2,4},{4,6},{6,7},{7,5},{5,3},{3,1},{1,0},{8,9},{10,8},{12,1... | collective-permute-start | bytes 1179656 | tf_op jit(solution)/shard_map/ppermute | solution.py:334
  12.9 1.6 %collective-permute-start.3 = (bf16[2,32,3072]{2,1,0:T(8,128)(2,1)S(1)}, bf16[2,32,3072]{2,1,0:T(8,128)(2,1)S(1)}, u32[]{:S(2)}, u32[]{:S(2)}) collective-permute-start(bf16[2,32,3072]{2,1,0:T(8,128)(2,1)S(1)} %pad_maximum_fusion), channel_id=1, source_target_pairs={{0,2},{2,4},{4,6},{6,7},{7,5},{5,3},{3,1},{1,0},{8,9},{10,8},{12,1... | collective-permute-start | bytes 1179656 | tf_op jit(solution)/shard_map/ppermute | solution.py:334
  14.5 3.4 %collective-permute-done.4 = bf16[2,32,3072]{2,1,0:T(8,128)(2,1)S(1)} collective-permute-done((bf16[2,32,3072]{2,1,0:T(8,128)(2,1)S(1)}, bf16[2,32,3072]{2,1,0:T(8,128)(2,1)S(1)}, u32[]{:S(2)}, u32[]{:S(2)}) %collective-permute-start.4) | collective-permute-done | bytes 393248 | tf_op jit(solution)/shard_map/ppermute | solution.py:334
  18.1 4.1 %collective-permute-done.3 = bf16[2,32,3072]{2,1,0:T(8,128)(2,1)S(1)} collective-permute-done((bf16[2,32,3072]{2,1,0:T(8,128)(2,1)S(1)}, bf16[2,32,3072]{2,1,0:T(8,128)(2,1)S(1)}, u32[]{:S(2)}, u32[]{:S(2)}) %collective-permute-start.3) | collective-permute-done | bytes 393248 | tf_op jit(solution)/shard_map/ppermute | solution.py:334
  22.3 2.1 %collective-permute-start.7 = (bf16[2,32,3072]{2,1,0:T(8,128)(2,1)S(1)}, bf16[2,32,3072]{2,1,0:T(8,128)(2,1)S(1)}, u32[]{:S(2)}, u32[]{:S(2)}) collective-permute-start(bf16[2,32,3072]{2,1,0:T(8,128)(2,1)S(1)} %collective-permute-done.3), channel_id=1, source_target_pairs={{0,2},{2,4},{4,6},{6,7},{7,5},{5,3},{3,1},{1,0},{8,9},{10,8},{12,1... | collective-permute-start | bytes 1179656 | tf_op jit(solution)/shard_map/ppermute | solution.py:334
  24.4 0.7 compare_select_fusion.7.refs_0_
  25.1 0.6 reshape.169.active_ref
  25.7 3.4 %tables.1 = (s32[25]{0:T(128)}, s32[3,28]{1,0:T(4,128)}, s32[2]{0:T(128)}) custom-call(s32[1]{0:T(128)} %bitcast.2.first_ref, s32[192]{0:T(256)} %reshape.169.active_ref), custom_call_target="tpu_custom_call" | custom-call | tf_op jit(solution)/shard_map/tables/pallas_call | solution.py:74
  29.1 1.6 %collective-permute-start.8 = (bf16[2,32,3072]{2,1,0:T(8,128)(2,1)S(1)}, bf16[2,32,3072]{2,1,0:T(8,128)(2,1)S(1)}, u32[]{:S(2)}, u32[]{:S(2)}) collective-permute-start(bf16[2,32,3072]{2,1,0:T(8,128)(2,1)S(1)} %collective-permute-done.4), channel_id=1, source_target_pairs={{0,2},{2,4},{4,6},{6,7},{7,5},{5,3},{3,1},{1,0},{8,9},{10,8},{12,1... | collective-permute-start | bytes 1179656 | tf_op jit(solution)/shard_map/ppermute | solution.py:334
  30.9 6.0 %collective-permute-done.8 = bf16[2,32,3072]{2,1,0:T(8,128)(2,1)S(1)} collective-permute-done((bf16[2,32,3072]{2,1,0:T(8,128)(2,1)S(1)}, bf16[2,32,3072]{2,1,0:T(8,128)(2,1)S(1)}, u32[]{:S(2)}, u32[]{:S(2)}) %collective-permute-start.8) | collective-permute-done | bytes 393248 | tf_op jit(solution)/shard_map/ppermute | solution.py:334
  37.0 1.6 %collective-permute-start.11 = (bf16[2,32,3072]{2,1,0:T(8,128)(2,1)S(1)}, bf16[2,32,3072]{2,1,0:T(8,128)(2,1)S(1)}, u32[]{:S(2)}, u32[]{:S(2)}) collective-permute-start(bf16[2,32,3072]{2,1,0:T(8,128)(2,1)S(1)} %collective-permute-done.7), channel_id=1, source_target_pairs={{0,2},{2,4},{4,6},{6,7},{7,5},{5,3},{3,1},{1,0},{8,9},{10,8},{12,1... | collective-permute-start | bytes 1179656 | tf_op jit(solution)/shard_map/ppermute | solution.py:334
  38.7 1.6 %collective-permute-start.12 = (bf16[2,32,3072]{2,1,0:T(8,128)(2,1)S(1)}, bf16[2,32,3072]{2,1,0:T(8,128)(2,1)S(1)}, u32[]{:S(2)}, u32[]{:S(2)}) collective-permute-start(bf16[2,32,3072]{2,1,0:T(8,128)(2,1)S(1)} %collective-permute-done.8), channel_id=1, source_target_pairs={{0,2},{2,4},{4,6},{6,7},{7,5},{5,3},{3,1},{1,0},{8,9},{10,8},{12,1... | collective-permute-start | bytes 1179656 | tf_op jit(solution)/shard_map/ppermute | solution.py:334
  40.4 4.4 %collective-permute-done.11 = bf16[2,32,3072]{2,1,0:T(8,128)(2,1)S(1)} collective-permute-done((bf16[2,32,3072]{2,1,0:T(8,128)(2,1)S(1)}, bf16[2,32,3072]{2,1,0:T(8,128)(2,1)S(1)}, u32[]{:S(2)}, u32[]{:S(2)}) %collective-permute-start.11) | collective-permute-done | bytes 393248 | tf_op jit(solution)/shard_map/ppermute | solution.py:334
  45.0 4.1 %collective-permute-done.12 = bf16[2,32,3072]{2,1,0:T(8,128)(2,1)S(1)} collective-permute-done((bf16[2,32,3072]{2,1,0:T(8,128)(2,1)S(1)}, bf16[2,32,3072]{2,1,0:T(8,128)(2,1)S(1)}, u32[]{:S(2)}, u32[]{:S(2)}) %collective-permute-start.12) | collective-permute-done | bytes 393248 | tf_op jit(solution)/shard_map/ppermute | solution.py:334
  49.2 1.6 %collective-permute-start.15 = (bf16[32,3072]{1,0:T(8,128)(2,1)S(1)}, bf16[32,3072]{1,0:T(8,128)(2,1)S(1)}, u32[]{:S(2)}, u32[]{:S(2)}) collective-permute-start(bf16[32,3072]{1,0:T(8,128)(2,1)S(1)} %get-tuple-element.41), channel_id=1, source_target_pairs={{0,2},{2,4},{4,6},{6,7},{7,5},{5,3},{3,1},{1,0},{8,9},{10,8},{12,1... | collective-permute-start | bytes 589832 | tf_op jit(solution)/shard_map/ppermute | solution.py:334
  50.8 1.6 %collective-permute-start.16 = (bf16[32,3072]{1,0:T(8,128)(2,1)S(1)}, bf16[32,3072]{1,0:T(8,128)(2,1)S(1)}, u32[]{:S(2)}, u32[]{:S(2)}) collective-permute-start(bf16[32,3072]{1,0:T(8,128)(2,1)S(1)} %get-tuple-element.44), channel_id=1, source_target_pairs={{0,2},{2,4},{4,6},{6,7},{7,5},{5,3},{3,1},{1,0},{8,9},{10,8},{12,1... | collective-permute-start | bytes 589832 | tf_op jit(solution)/shard_map/ppermute | solution.py:334
  52.5 2.4 %collective-permute-done.15 = bf16[32,3072]{1,0:T(8,128)(2,1)S(1)} collective-permute-done((bf16[32,3072]{1,0:T(8,128)(2,1)S(1)}, bf16[32,3072]{1,0:T(8,128)(2,1)S(1)}, u32[]{:S(2)}, u32[]{:S(2)}) %collective-permute-start.15) | collective-permute-done | bytes 196640 | tf_op jit(solution)/shard_map/ppermute | solution.py:334
  54.9 2.1 %collective-permute-done.16 = bf16[32,3072]{1,0:T(8,128)(2,1)S(1)} collective-permute-done((bf16[32,3072]{1,0:T(8,128)(2,1)S(1)}, bf16[32,3072]{1,0:T(8,128)(2,1)S(1)}, u32[]{:S(2)}, u32[]{:S(2)}) %collective-permute-start.16) | collective-permute-done | bytes 196640 | tf_op jit(solution)/shard_map/ppermute | solution.py:334
  57.1 11.0 %up.1 = (f32[12,128,128]{2,1,0:T(8,128)S(1)}, bf16[12,128,128]{2,1,0:T(8,128)(2,1)S(1)}) custom-call(s32[8]{0:T(128)S(1)} %compare_select_fusion.7.refs_0_, s32[1]{0:T(128)} %bitcast.1.refs_1_, s32[25]{0:T(128)S(1)} %copy-done.3, s32[3,28]{1,0:T(4,128)S(1)} %copy-done.2, s32[2]{0:T(128)S(1)} %copy-done.4, bf16[3072,3072]{1,0:T(8,128)(2,1)} %refs_5_.2, ...), custom_call_target="tpu_custom_call" | custom-call | flops 2415919104 | bytes 18874368 | tf_op jit(solution)/shard_map/up/pallas_call | solution.py:152
  68.2 1.7 %collective-permute-done.17 = bf16[12,128,128]{2,1,0:T(8,128)(2,1)S(1)} collective-permute-done((bf16[12,128,128]{2,1,0:T(8,128)(2,1)S(1)}, bf16[12,128,128]{2,1,0:T(8,128)(2,1)S(1)}, u32[]{:S(2)}, u32[]{:S(2)}) %collective-permute-start.17) | collective-permute-done | bytes 393248 | tf_op jit(solution)/shard_map/ppermute | solution.py:331
  70.1 1.6 %collective-permute-start.18 = (bf16[12,128,128]{2,1,0:T(8,128)(2,1)S(1)}, bf16[12,128,128]{2,1,0:T(8,128)(2,1)S(1)}, u32[]{:S(2)}, u32[]{:S(2)}) collective-permute-start(bf16[12,128,128]{2,1,0:T(8,128)(2,1)S(1)} %fusion), channel_id=1, source_target_pairs={{0,16},{8,24},{16,0},{24,8},{1,17},{9,25},{17,1},{25,9},{2,18},{10... | collective-permute-start | bytes 1179656 | tf_op jit(solution)/shard_map/ppermute | solution.py:338
  72.3 9.0 %collective-permute-done.18 = bf16[12,128,128]{2,1,0:T(8,128)(2,1)S(1)} collective-permute-done((bf16[12,128,128]{2,1,0:T(8,128)(2,1)S(1)}, bf16[12,128,128]{2,1,0:T(8,128)(2,1)S(1)}, u32[]{:S(2)}, u32[]{:S(2)}) %collective-permute-start.18) | collective-permute-done | bytes 393248 | tf_op jit(solution)/shard_map/ppermute | solution.py:338
  81.5 1.7 %collective-permute-done.19.refs_7_ = bf16[12,128,128]{2,1,0:T(8,128)(2,1)S(1)} collective-permute-done((bf16[12,128,128]{2,1,0:T(8,128)(2,1)S(1)}, bf16[12,128,128]{2,1,0:T(8,128)(2,1)S(1)}, u32[]{:S(2)}, u32[]{:S(2)}) %collective-permute-start.19) | collective-permute-done | bytes 393248 | tf_op jit(solution)/shard_map/ppermute | solution.py:331
  83.3 11.5 %down.1 = (bf16[2,32,3072]{2,1,0:T(8,128)(2,1)S(1)}, bf16[3,2,32,3072]{3,2,1,0:T(8,128)(2,1)S(1)}, bf16[3,2,32,3072]{3,2,1,0:T(8,128)(2,1)S(1)}, bf16[2,32,3072]{2,1,0:T(8,128)(2,1)S(1)}) custom-call(s32[8]{0:T(128)S(1)} %compare_select_fusion.7.refs_0_, s32[1]{0:T(128)} %bitcast.1.refs_1_, s32[25]{0:T(128)S(1)} %copy-done.3, s32[3,28]{1,0:T(4,128)S(1)} %copy-done.2, ...), custom_call_target="tpu_custom_call" | custom-call | flops 2415919104 | bytes 18874368 | tf_op jit(solution)/shard_map/down/pallas_call | solution.py:288
  95.0 1.6 %collective-permute-start.20 = (bf16[32,3072]{1,0:T(8,128)(2,1)S(1)}, bf16[32,3072]{1,0:T(8,128)(2,1)S(1)}, u32[]{:S(2)}, u32[]{:S(2)}) collective-permute-start(bf16[32,3072]{1,0:T(8,128)(2,1)S(1)} %get-tuple-element.39), channel_id=1, source_target_pairs={{0,2},{2,4},{4,6},{6,7},{7,5},{5,3},{3,1},{1,0},{8,9},{10,8},{12,1... | collective-permute-start | bytes 589832 | tf_op jit(solution)/shard_map/ppermute | solution.py:334
  96.7 1.6 %collective-permute-start.26 = (bf16[32,3072]{1,0:T(8,128)(2,1)S(1)}, bf16[32,3072]{1,0:T(8,128)(2,1)S(1)}, u32[]{:S(2)}, u32[]{:S(2)}) collective-permute-start(bf16[32,3072]{1,0:T(8,128)(2,1)S(1)} %get-tuple-element.40), channel_id=1, source_target_pairs={{0,2},{2,4},{4,6},{6,7},{7,5},{5,3},{3,1},{1,0},{8,9},{10,8},{12,1... | collective-permute-start | bytes 589832 | tf_op jit(solution)/shard_map/ppermute | solution.py:334
  98.3 2.5 %collective-permute-done.20 = bf16[32,3072]{1,0:T(8,128)(2,1)S(1)} collective-permute-done((bf16[32,3072]{1,0:T(8,128)(2,1)S(1)}, bf16[32,3072]{1,0:T(8,128)(2,1)S(1)}, u32[]{:S(2)}, u32[]{:S(2)}) %collective-permute-start.20) | collective-permute-done | bytes 196640 | tf_op jit(solution)/shard_map/ppermute | solution.py:334
  100.8 2.1 %collective-permute-done.26 = bf16[32,3072]{1,0:T(8,128)(2,1)S(1)} collective-permute-done((bf16[32,3072]{1,0:T(8,128)(2,1)S(1)}, bf16[32,3072]{1,0:T(8,128)(2,1)S(1)}, u32[]{:S(2)}, u32[]{:S(2)}) %collective-permute-start.26) | collective-permute-done | bytes 196640 | tf_op jit(solution)/shard_map/ppermute | solution.py:334
  103.1 1.6 %collective-permute-start.27 = (bf16[2,32,3072]{2,1,0:T(8,128)(2,1)S(1)}, bf16[2,32,3072]{2,1,0:T(8,128)(2,1)S(1)}, u32[]{:S(2)}, u32[]{:S(2)}) collective-permute-start(bf16[2,32,3072]{2,1,0:T(8,128)(2,1)S(1)} %pad_maximum_fusion.10), channel_id=1, source_target_pairs={{0,2},{2,4},{4,6},{6,7},{7,5},{5,3},{3,1},{1,0},{8,9},{10,8},{12,1... | collective-permute-start | bytes 1179656 | tf_op jit(solution)/shard_map/ppermute | solution.py:334
  104.9 1.6 %collective-permute-start.22 = (bf16[2,32,3072]{2,1,0:T(8,128)(2,1)S(1)}, bf16[2,32,3072]{2,1,0:T(8,128)(2,1)S(1)}, u32[]{:S(2)}, u32[]{:S(2)}) collective-permute-start(bf16[2,32,3072]{2,1,0:T(8,128)(2,1)S(1)} %pad_maximum_fusion.9), channel_id=1, source_target_pairs={{0,2},{2,4},{4,6},{6,7},{7,5},{5,3},{3,1},{1,0},{8,9},{10,8},{12,1... | collective-permute-start | bytes 1179656 | tf_op jit(solution)/shard_map/ppermute | solution.py:334
  106.5 4.5 %collective-permute-done.27 = bf16[2,32,3072]{2,1,0:T(8,128)(2,1)S(1)} collective-permute-done((bf16[2,32,3072]{2,1,0:T(8,128)(2,1)S(1)}, bf16[2,32,3072]{2,1,0:T(8,128)(2,1)S(1)}, u32[]{:S(2)}, u32[]{:S(2)}) %collective-permute-start.27) | collective-permute-done | bytes 393248 | tf_op jit(solution)/shard_map/ppermute | solution.py:334
  111.1 1.6 %collective-permute-start.28 = (bf16[2,32,3072]{2,1,0:T(8,128)(2,1)S(1)}, bf16[2,32,3072]{2,1,0:T(8,128)(2,1)S(1)}, u32[]{:S(2)}, u32[]{:S(2)}) collective-permute-start(bf16[2,32,3072]{2,1,0:T(8,128)(2,1)S(1)} %add_convert_fusion.1), channel_id=1, source_target_pairs={{0,2},{2,4},{4,6},{6,7},{7,5},{5,3},{3,1},{1,0},{8,9},{10,8},{12,1... | collective-permute-start | bytes 1179656 | tf_op jit(solution)/shard_map/ppermute | solution.py:334
  112.7 2.5 %collective-permute-done.22 = bf16[2,32,3072]{2,1,0:T(8,128)(2,1)S(1)} collective-permute-done((bf16[2,32,3072]{2,1,0:T(8,128)(2,1)S(1)}, bf16[2,32,3072]{2,1,0:T(8,128)(2,1)S(1)}, u32[]{:S(2)}, u32[]{:S(2)}) %collective-permute-start.22) | collective-permute-done | bytes 393248 | tf_op jit(solution)/shard_map/ppermute | solution.py:334
  115.3 1.6 %collective-permute-start.23 = (bf16[2,32,3072]{2,1,0:T(8,128)(2,1)S(1)}, bf16[2,32,3072]{2,1,0:T(8,128)(2,1)S(1)}, u32[]{:S(2)}, u32[]{:S(2)}) collective-permute-start(bf16[2,32,3072]{2,1,0:T(8,128)(2,1)S(1)} %add_convert_fusion.3), channel_id=1, source_target_pairs={{0,2},{2,4},{4,6},{6,7},{7,5},{5,3},{3,1},{1,0},{8,9},{10,8},{12,1... | collective-permute-start | bytes 1179656 | tf_op jit(solution)/shard_map/ppermute | solution.py:334
  116.9 2.5 %collective-permute-done.28 = bf16[2,32,3072]{2,1,0:T(8,128)(2,1)S(1)} collective-permute-done((bf16[2,32,3072]{2,1,0:T(8,128)(2,1)S(1)}, bf16[2,32,3072]{2,1,0:T(8,128)(2,1)S(1)}, u32[]{:S(2)}, u32[]{:S(2)}) %collective-permute-start.28) | collective-permute-done | bytes 393248 | tf_op jit(solution)/shard_map/ppermute | solution.py:334
  119.5 1.6 %collective-permute-start.29 = (bf16[2,32,3072]{2,1,0:T(8,128)(2,1)S(1)}, bf16[2,32,3072]{2,1,0:T(8,128)(2,1)S(1)}, u32[]{:S(2)}, u32[]{:S(2)}) collective-permute-start(bf16[2,32,3072]{2,1,0:T(8,128)(2,1)S(1)} %add_convert_fusion), channel_id=1, source_target_pairs={{0,2},{2,4},{4,6},{6,7},{7,5},{5,3},{3,1},{1,0},{8,9},{10,8},{12,1... | collective-permute-start | bytes 1179656 | tf_op jit(solution)/shard_map/ppermute | solution.py:334
  121.1 2.5 %collective-permute-done.23 = bf16[2,32,3072]{2,1,0:T(8,128)(2,1)S(1)} collective-permute-done((bf16[2,32,3072]{2,1,0:T(8,128)(2,1)S(1)}, bf16[2,32,3072]{2,1,0:T(8,128)(2,1)S(1)}, u32[]{:S(2)}, u32[]{:S(2)}) %collective-permute-start.23) | collective-permute-done | bytes 393248 | tf_op jit(solution)/shard_map/ppermute | solution.py:334
  123.7 1.6 %collective-permute-start.24 = (bf16[2,32,3072]{2,1,0:T(8,128)(2,1)S(1)}, bf16[2,32,3072]{2,1,0:T(8,128)(2,1)S(1)}, u32[]{:S(2)}, u32[]{:S(2)}) collective-permute-start(bf16[2,32,3072]{2,1,0:T(8,128)(2,1)S(1)} %add_convert_fusion.2), channel_id=1, source_target_pairs={{0,2},{2,4},{4,6},{6,7},{7,5},{5,3},{3,1},{1,0},{8,9},{10,8},{12,1... | collective-permute-start | bytes 1179656 | tf_op jit(solution)/shard_map/ppermute | solution.py:334
  125.3 2.5 %collective-permute-done.29 = bf16[2,32,3072]{2,1,0:T(8,128)(2,1)S(1)} collective-permute-done((bf16[2,32,3072]{2,1,0:T(8,128)(2,1)S(1)}, bf16[2,32,3072]{2,1,0:T(8,128)(2,1)S(1)}, u32[]{:S(2)}, u32[]{:S(2)}) %collective-permute-start.29) | collective-permute-done | bytes 393248 | tf_op jit(solution)/shard_map/ppermute | solution.py:334
  127.9 4.1 %collective-permute-done.24 = bf16[2,32,3072]{2,1,0:T(8,128)(2,1)S(1)} collective-permute-done((bf16[2,32,3072]{2,1,0:T(8,128)(2,1)S(1)}, bf16[2,32,3072]{2,1,0:T(8,128)(2,1)S(1)}, u32[]{:S(2)}, u32[]{:S(2)}) %collective-permute-start.24) | collective-permute-done | bytes 393248 | tf_op jit(solution)/shard_map/ppermute | solution.py:334
  132.2 1.3 %collective-permute-done.25 = bf16[32,3072]{1,0:T(8,128)(2,1)S(1)} collective-permute-done((bf16[32,3072]{1,0:T(8,128)(2,1)S(1)}, bf16[32,3072]{1,0:T(8,128)(2,1)S(1)}, u32[]{:S(2)}, u32[]{:S(2)}) %collective-permute-start.25) | collective-permute-done | bytes 196640 | tf_op jit(solution)/shard_map/ppermute | solution.py:331
  133.8 0.8 pad_maximum_fusion.11
  (81 shorter events, 4.7 us)
Async XLA Ops:
  0.0 71.7 %copy-start = (f32[3072]{0:T(1024)S(1)}, f32[3072]{0:T(1024)}, u32[]{:S(2)}) copy-start(f32[3072]{0:T(1024)} %param.14) | copy-start | bytes 36868
  1.2 1.4 %collective-permute-start = (f32[2,2,32]{2,1,0:T(2,128)S(1)}, f32[2,2,32]{2,1,0:T(2,128)S(1)}, u32[]{:S(2)}, u32[]{:S(2)}) collective-permute-start(f32[2,2,32]{2,1,0:T(2,128)S(1)} %pad_maximum_fusion.12), channel_id=1, source_target_pairs={{0,8},{8,0},{16,24},{24,16},{1,9},{9,1},{17,25},{25,17},{2,10},{10... | collective-permute-start | bytes 1544 | tf_op jit(solution)/shard_map/ppermute | solution.py:331
  2.6 4.4 %collective-permute-start.1 = (f32[2,2,32]{2,1,0:T(2,128)S(1)}, f32[2,2,32]{2,1,0:T(2,128)S(1)}, u32[]{:S(2)}, u32[]{:S(2)}) collective-permute-start(f32[2,2,32]{2,1,0:T(2,128)S(1)} %fusion.20), channel_id=1, source_target_pairs={{0,16},{8,24},{16,0},{24,8},{1,17},{9,25},{17,1},{25,9},{2,18},{10... | collective-permute-start | bytes 1544 | tf_op jit(solution)/shard_map/ppermute | solution.py:338
  8.2 4.0 %copy-start.8 = (s32[8]{0:T(128)S(1)}, s32[8]{0:T(128)}, u32[]{:S(2)}) copy-start(s32[8]{0:T(128)} %constant.69.clone) | copy-start | bytes 100
  8.2 1.8 %collective-permute-start.2 = (bf16[2,32,3072]{2,1,0:T(8,128)(2,1)S(1)}, bf16[2,32,3072]{2,1,0:T(8,128)(2,1)S(1)}, u32[]{:S(2)}, u32[]{:S(2)}) collective-permute-start(bf16[2,32,3072]{2,1,0:T(8,128)(2,1)S(1)} %add_convert_fusion.4.refs_6_), channel_id=1, source_target_pairs={{0,8},{8,0},{16,24},{24,16},{1,9},{9,1},{17,25},{25,17},{2,10},{10... | collective-permute-start | bytes 1179656 | tf_op jit(solution)/shard_map/ppermute | solution.py:331
  10.1 7.9 %collective-permute-start.4 = (bf16[2,32,3072]{2,1,0:T(8,128)(2,1)S(1)}, bf16[2,32,3072]{2,1,0:T(8,128)(2,1)S(1)}, u32[]{:S(2)}, u32[]{:S(2)}) collective-permute-start(bf16[2,32,3072]{2,1,0:T(8,128)(2,1)S(1)} %pad_maximum_fusion.1), channel_id=1, source_target_pairs={{0,2},{2,4},{4,6},{6,7},{7,5},{5,3},{3,1},{1,0},{8,9},{10,8},{12,1... | collective-permute-start | bytes 1179656 | tf_op jit(solution)/shard_map/ppermute | solution.py:334
  12.8 12.2 %copy-start.7 = (s32[2,2,48]{2,1,0:T(2,128)S(1)}, s32[2,2,48]{2,1,0:T(2,128)}, u32[]{:S(2)}) copy-start(s32[2,2,48]{2,1,0:T(2,128)} %param.17) | copy-start | bytes 2308
  12.9 9.3 %collective-permute-start.3 = (bf16[2,32,3072]{2,1,0:T(8,128)(2,1)S(1)}, bf16[2,32,3072]{2,1,0:T(8,128)(2,1)S(1)}, u32[]{:S(2)}, u32[]{:S(2)}) collective-permute-start(bf16[2,32,3072]{2,1,0:T(8,128)(2,1)S(1)} %pad_maximum_fusion), channel_id=1, source_target_pairs={{0,2},{2,4},{4,6},{6,7},{7,5},{5,3},{3,1},{1,0},{8,9},{10,8},{12,1... | collective-permute-start | bytes 1179656 | tf_op jit(solution)/shard_map/ppermute | solution.py:334
  18.0 12.7 %collective-permute-start.6 = (bf16[32,3072]{1,0:T(8,128)(2,1)S(1)}, bf16[32,3072]{1,0:T(8,128)(2,1)S(1)}, u32[]{:S(2)}, u32[]{:S(2)}) collective-permute-start(bf16[32,3072]{1,0:T(8,128)(2,1)S(1)} %get-tuple-element.53), channel_id=1, source_target_pairs={{0,8},{8,0},{16,24},{24,16},{1,9},{9,1},{17,25},{25,17},{2,10},{10... | collective-permute-start | bytes 589832 | tf_op jit(solution)/shard_map/ppermute | solution.py:331
  22.2 8.5 %collective-permute-start.5 = (bf16[32,3072]{1,0:T(8,128)(2,1)S(1)}, bf16[32,3072]{1,0:T(8,128)(2,1)S(1)}, u32[]{:S(2)}, u32[]{:S(2)}) collective-permute-start(bf16[32,3072]{1,0:T(8,128)(2,1)S(1)} %get-tuple-element.51), channel_id=1, source_target_pairs={{0,8},{8,0},{16,24},{24,16},{1,9},{9,1},{17,25},{25,17},{2,10},{10... | collective-permute-start | bytes 589832 | tf_op jit(solution)/shard_map/ppermute | solution.py:331
  22.3 8.5 %collective-permute-start.7 = (bf16[2,32,3072]{2,1,0:T(8,128)(2,1)S(1)}, bf16[2,32,3072]{2,1,0:T(8,128)(2,1)S(1)}, u32[]{:S(2)}, u32[]{:S(2)}) collective-permute-start(bf16[2,32,3072]{2,1,0:T(8,128)(2,1)S(1)} %collective-permute-done.3), channel_id=1, source_target_pairs={{0,2},{2,4},{4,6},{6,7},{7,5},{5,3},{3,1},{1,0},{8,9},{10,8},{12,1... | collective-permute-start | bytes 1179656 | tf_op jit(solution)/shard_map/ppermute | solution.py:334
  29.1 7.8 %collective-permute-start.8 = (bf16[2,32,3072]{2,1,0:T(8,128)(2,1)S(1)}, bf16[2,32,3072]{2,1,0:T(8,128)(2,1)S(1)}, u32[]{:S(2)}, u32[]{:S(2)}) collective-permute-start(bf16[2,32,3072]{2,1,0:T(8,128)(2,1)S(1)} %collective-permute-done.4), channel_id=1, source_target_pairs={{0,2},{2,4},{4,6},{6,7},{7,5},{5,3},{3,1},{1,0},{8,9},{10,8},{12,1... | collective-permute-start | bytes 1179656 | tf_op jit(solution)/shard_map/ppermute | solution.py:334
  30.8 9.5 %collective-permute-start.9 = (bf16[32,3072]{1,0:T(8,128)(2,1)S(1)}, bf16[32,3072]{1,0:T(8,128)(2,1)S(1)}, u32[]{:S(2)}, u32[]{:S(2)}) collective-permute-start(bf16[32,3072]{1,0:T(8,128)(2,1)S(1)} %get-tuple-element.47), channel_id=1, source_target_pairs={{0,8},{8,0},{16,24},{24,16},{1,9},{9,1},{17,25},{25,17},{2,10},{10... | collective-permute-start | bytes 589832 | tf_op jit(solution)/shard_map/ppermute | solution.py:331
  37.0 3.4 %collective-permute-start.10 = (bf16[32,3072]{1,0:T(8,128)(2,1)S(1)}, bf16[32,3072]{1,0:T(8,128)(2,1)S(1)}, u32[]{:S(2)}, u32[]{:S(2)}) collective-permute-start(bf16[32,3072]{1,0:T(8,128)(2,1)S(1)} %get-tuple-element.49), channel_id=1, source_target_pairs={{0,8},{8,0},{16,24},{24,16},{1,9},{9,1},{17,25},{25,17},{2,10},{10... | collective-permute-start | bytes 589832 | tf_op jit(solution)/shard_map/ppermute | solution.py:331
  37.0 7.8 %collective-permute-start.11 = (bf16[2,32,3072]{2,1,0:T(8,128)(2,1)S(1)}, bf16[2,32,3072]{2,1,0:T(8,128)(2,1)S(1)}, u32[]{:S(2)}, u32[]{:S(2)}) collective-permute-start(bf16[2,32,3072]{2,1,0:T(8,128)(2,1)S(1)} %collective-permute-done.7), channel_id=1, source_target_pairs={{0,2},{2,4},{4,6},{6,7},{7,5},{5,3},{3,1},{1,0},{8,9},{10,8},{12,1... | collective-permute-start | bytes 1179656 | tf_op jit(solution)/shard_map/ppermute | solution.py:334
  38.7 10.3 %collective-permute-start.12 = (bf16[2,32,3072]{2,1,0:T(8,128)(2,1)S(1)}, bf16[2,32,3072]{2,1,0:T(8,128)(2,1)S(1)}, u32[]{:S(2)}, u32[]{:S(2)}) collective-permute-start(bf16[2,32,3072]{2,1,0:T(8,128)(2,1)S(1)} %collective-permute-done.8), channel_id=1, source_target_pairs={{0,2},{2,4},{4,6},{6,7},{7,5},{5,3},{3,1},{1,0},{8,9},{10,8},{12,1... | collective-permute-start | bytes 1179656 | tf_op jit(solution)/shard_map/ppermute | solution.py:334
  44.9 7.6 %collective-permute-start.13 = (bf16[32,3072]{1,0:T(8,128)(2,1)S(1)}, bf16[32,3072]{1,0:T(8,128)(2,1)S(1)}, u32[]{:S(2)}, u32[]{:S(2)}) collective-permute-start(bf16[32,3072]{1,0:T(8,128)(2,1)S(1)} %get-tuple-element.42), channel_id=1, source_target_pairs={{0,8},{8,0},{16,24},{24,16},{1,9},{9,1},{17,25},{25,17},{2,10},{10... | collective-permute-start | bytes 589832 | tf_op jit(solution)/shard_map/ppermute | solution.py:331
  49.1 3.3 %collective-permute-start.14 = (bf16[32,3072]{1,0:T(8,128)(2,1)S(1)}, bf16[32,3072]{1,0:T(8,128)(2,1)S(1)}, u32[]{:S(2)}, u32[]{:S(2)}) collective-permute-start(bf16[32,3072]{1,0:T(8,128)(2,1)S(1)} %get-tuple-element.45), channel_id=1, source_target_pairs={{0,8},{8,0},{16,24},{24,16},{1,9},{9,1},{17,25},{25,17},{2,10},{10... | collective-permute-start | bytes 589832 | tf_op jit(solution)/shard_map/ppermute | solution.py:331
  49.2 5.7 %collective-permute-start.15 = (bf16[32,3072]{1,0:T(8,128)(2,1)S(1)}, bf16[32,3072]{1,0:T(8,128)(2,1)S(1)}, u32[]{:S(2)}, u32[]{:S(2)}) collective-permute-start(bf16[32,3072]{1,0:T(8,128)(2,1)S(1)} %get-tuple-element.41), channel_id=1, source_target_pairs={{0,2},{2,4},{4,6},{6,7},{7,5},{5,3},{3,1},{1,0},{8,9},{10,8},{12,1... | collective-permute-start | bytes 589832 | tf_op jit(solution)/shard_map/ppermute | solution.py:334
  50.8 6.2 %collective-permute-start.16 = (bf16[32,3072]{1,0:T(8,128)(2,1)S(1)}, bf16[32,3072]{1,0:T(8,128)(2,1)S(1)}, u32[]{:S(2)}, u32[]{:S(2)}) collective-permute-start(bf16[32,3072]{1,0:T(8,128)(2,1)S(1)} %get-tuple-element.44), channel_id=1, source_target_pairs={{0,2},{2,4},{4,6},{6,7},{7,5},{5,3},{3,1},{1,0},{8,9},{10,8},{12,1... | collective-permute-start | bytes 589832 | tf_op jit(solution)/shard_map/ppermute | solution.py:334
  52.4 4.7 %copy-start.2 = (s32[3,28]{1,0:T(4,128)S(1)}, s32[3,28]{1,0:T(4,128)}, u32[]{:S(2)}) copy-start(s32[3,28]{1,0:T(4,128)} %get-tuple-element.15.refs_3_) | copy-start | bytes 1012
  52.4 4.7 %copy-start.3 = (s32[25]{0:T(128)S(1)}, s32[25]{0:T(128)}, u32[]{:S(2)}) copy-start(s32[25]{0:T(128)} %get-tuple-element.14.refs_2_) | copy-start | bytes 304
  52.4 4.7 %copy-start.4 = (s32[2]{0:T(128)S(1)}, s32[2]{0:T(128)}, u32[]{:S(2)}) copy-start(s32[2]{0:T(128)} %get-tuple-element.16.refs_4_) | copy-start | bytes 28
  68.2 1.8 %collective-permute-start.17 = (bf16[12,128,128]{2,1,0:T(8,128)(2,1)S(1)}, bf16[12,128,128]{2,1,0:T(8,128)(2,1)S(1)}, u32[]{:S(2)}, u32[]{:S(2)}) collective-permute-start(bf16[12,128,128]{2,1,0:T(8,128)(2,1)S(1)} %get-tuple-element.18), channel_id=1, source_target_pairs={{0,8},{8,0},{16,24},{24,16},{1,9},{9,1},{17,25},{25,17},{2,10},{10... | collective-permute-start | bytes 1179656 | tf_op jit(solution)/shard_map/ppermute | solution.py:331
  70.1 11.2 %collective-permute-start.18 = (bf16[12,128,128]{2,1,0:T(8,128)(2,1)S(1)}, bf16[12,128,128]{2,1,0:T(8,128)(2,1)S(1)}, u32[]{:S(2)}, u32[]{:S(2)}) collective-permute-start(bf16[12,128,128]{2,1,0:T(8,128)(2,1)S(1)} %fusion), channel_id=1, source_target_pairs={{0,16},{8,24},{16,0},{24,8},{1,17},{9,25},{17,1},{25,9},{2,18},{10... | collective-permute-start | bytes 1179656 | tf_op jit(solution)/shard_map/ppermute | solution.py:338
  81.5 1.8 %collective-permute-start.19 = (bf16[12,128,128]{2,1,0:T(8,128)(2,1)S(1)}, bf16[12,128,128]{2,1,0:T(8,128)(2,1)S(1)}, u32[]{:S(2)}, u32[]{:S(2)}) collective-permute-start(bf16[12,128,128]{2,1,0:T(8,128)(2,1)S(1)} %maximum_convert_fusion.refs_6_), channel_id=1, source_target_pairs={{0,8},{8,0},{16,24},{24,16},{1,9},{9,1},{17,25},{25,17},{2,10},{10... | collective-permute-start | bytes 1179656 | tf_op jit(solution)/shard_map/ppermute | solution.py:331
  94.8 8.2 %collective-permute-start.21 = (bf16[3,2,32,3072]{3,2,1,0:T(8,128)(2,1)S(1)}, bf16[3,2,32,3072]{3,2,1,0:T(8,128)(2,1)S(1)}, u32[]{:S(2)}, u32[]{:S(2)}) collective-permute-start(bf16[3,2,32,3072]{3,2,1,0:T(8,128)(2,1)S(1)} %get-tuple-element.22), channel_id=1, source_target_pairs={{0,8},{8,0},{16,24},{24,16},{1,9},{9,1},{17,25},{25,17},{2,10},{10... | collective-permute-start | bytes 3538952 | tf_op jit(solution)/shard_map/ppermute | solution.py:331
  95.0 5.7 %collective-permute-start.20 = (bf16[32,3072]{1,0:T(8,128)(2,1)S(1)}, bf16[32,3072]{1,0:T(8,128)(2,1)S(1)}, u32[]{:S(2)}, u32[]{:S(2)}) collective-permute-start(bf16[32,3072]{1,0:T(8,128)(2,1)S(1)} %get-tuple-element.39), channel_id=1, source_target_pairs={{0,2},{2,4},{4,6},{6,7},{7,5},{5,3},{3,1},{1,0},{8,9},{10,8},{12,1... | collective-permute-start | bytes 589832 | tf_op jit(solution)/shard_map/ppermute | solution.py:334
  96.7 6.2 %collective-permute-start.26 = (bf16[32,3072]{1,0:T(8,128)(2,1)S(1)}, bf16[32,3072]{1,0:T(8,128)(2,1)S(1)}, u32[]{:S(2)}, u32[]{:S(2)}) collective-permute-start(bf16[32,3072]{1,0:T(8,128)(2,1)S(1)} %get-tuple-element.40), channel_id=1, source_target_pairs={{0,2},{2,4},{4,6},{6,7},{7,5},{5,3},{3,1},{1,0},{8,9},{10,8},{12,1... | collective-permute-start | bytes 589832 | tf_op jit(solution)/shard_map/ppermute | solution.py:334
  103.1 7.8 %collective-permute-start.27 = (bf16[2,32,3072]{2,1,0:T(8,128)(2,1)S(1)}, bf16[2,32,3072]{2,1,0:T(8,128)(2,1)S(1)}, u32[]{:S(2)}, u32[]{:S(2)}) collective-permute-start(bf16[2,32,3072]{2,1,0:T(8,128)(2,1)S(1)} %pad_maximum_fusion.10), channel_id=1, source_target_pairs={{0,2},{2,4},{4,6},{6,7},{7,5},{5,3},{3,1},{1,0},{8,9},{10,8},{12,1... | collective-permute-start | bytes 1179656 | tf_op jit(solution)/shard_map/ppermute | solution.py:334
  104.9 10.3 %collective-permute-start.22 = (bf16[2,32,3072]{2,1,0:T(8,128)(2,1)S(1)}, bf16[2,32,3072]{2,1,0:T(8,128)(2,1)S(1)}, u32[]{:S(2)}, u32[]{:S(2)}) collective-permute-start(bf16[2,32,3072]{2,1,0:T(8,128)(2,1)S(1)} %pad_maximum_fusion.9), channel_id=1, source_target_pairs={{0,2},{2,4},{4,6},{6,7},{7,5},{5,3},{3,1},{1,0},{8,9},{10,8},{12,1... | collective-permute-start | bytes 1179656 | tf_op jit(solution)/shard_map/ppermute | solution.py:334
  111.1 8.3 %collective-permute-start.28 = (bf16[2,32,3072]{2,1,0:T(8,128)(2,1)S(1)}, bf16[2,32,3072]{2,1,0:T(8,128)(2,1)S(1)}, u32[]{:S(2)}, u32[]{:S(2)}) collective-permute-start(bf16[2,32,3072]{2,1,0:T(8,128)(2,1)S(1)} %add_convert_fusion.1), channel_id=1, source_target_pairs={{0,2},{2,4},{4,6},{6,7},{7,5},{5,3},{3,1},{1,0},{8,9},{10,8},{12,1... | collective-permute-start | bytes 1179656 | tf_op jit(solution)/shard_map/ppermute | solution.py:334
  115.3 8.3 %collective-permute-start.23 = (bf16[2,32,3072]{2,1,0:T(8,128)(2,1)S(1)}, bf16[2,32,3072]{2,1,0:T(8,128)(2,1)S(1)}, u32[]{:S(2)}, u32[]{:S(2)}) collective-permute-start(bf16[2,32,3072]{2,1,0:T(8,128)(2,1)S(1)} %add_convert_fusion.3), channel_id=1, source_target_pairs={{0,2},{2,4},{4,6},{6,7},{7,5},{5,3},{3,1},{1,0},{8,9},{10,8},{12,1... | collective-permute-start | bytes 1179656 | tf_op jit(solution)/shard_map/ppermute | solution.py:334
  119.5 12.6 %copy-start.5 = (bf16[2,32,3072]{2,1,0:T(8,128)(2,1)S(1)}, bf16[2,32,3072]{2,1,0:T(8,128)(2,1)}, u32[]{:S(2)}) copy-start(bf16[2,32,3072]{2,1,0:T(8,128)(2,1)} %param.10) | copy-start | bytes 1179652
  119.5 8.3 %collective-permute-start.29 = (bf16[2,32,3072]{2,1,0:T(8,128)(2,1)S(1)}, bf16[2,32,3072]{2,1,0:T(8,128)(2,1)S(1)}, u32[]{:S(2)}, u32[]{:S(2)}) collective-permute-start(bf16[2,32,3072]{2,1,0:T(8,128)(2,1)S(1)} %add_convert_fusion), channel_id=1, source_target_pairs={{0,2},{2,4},{4,6},{6,7},{7,5},{5,3},{3,1},{1,0},{8,9},{10,8},{12,1... | collective-permute-start | bytes 1179656 | tf_op jit(solution)/shard_map/ppermute | solution.py:334
  123.7 9.9 %copy-start.6 = (f32[3072]{0:T(1024)S(1)}, f32[3072]{0:T(1024)}, u32[]{:S(2)}) copy-start(f32[3072]{0:T(1024)} %param.16) | copy-start | bytes 36868
  123.7 8.3 %collective-permute-start.24 = (bf16[2,32,3072]{2,1,0:T(8,128)(2,1)S(1)}, bf16[2,32,3072]{2,1,0:T(8,128)(2,1)S(1)}, u32[]{:S(2)}, u32[]{:S(2)}) collective-permute-start(bf16[2,32,3072]{2,1,0:T(8,128)(2,1)S(1)} %add_convert_fusion.2), channel_id=1, source_target_pairs={{0,2},{2,4},{4,6},{6,7},{7,5},{5,3},{3,1},{1,0},{8,9},{10,8},{12,1... | collective-permute-start | bytes 1179656 | tf_op jit(solution)/shard_map/ppermute | solution.py:334
  127.8 4.4 %collective-permute-start.30 = (bf16[32,3072]{1,0:T(8,128)(2,1)S(1)}, bf16[32,3072]{1,0:T(8,128)(2,1)S(1)}, u32[]{:S(2)}, u32[]{:S(2)}) collective-permute-start(bf16[32,3072]{1,0:T(8,128)(2,1)S(1)} %slice_bitcast_fusion.2), channel_id=1, source_target_pairs={{0,8},{8,0},{16,24},{24,16},{1,9},{9,1},{17,25},{25,17},{2,10},{10... | collective-permute-start | bytes 589832 | tf_op jit(solution)/shard_map/ppermute | solution.py:331
  132.1 1.5 %collective-permute-start.25 = (bf16[32,3072]{1,0:T(8,128)(2,1)S(1)}, bf16[32,3072]{1,0:T(8,128)(2,1)S(1)}, u32[]{:S(2)}, u32[]{:S(2)}) collective-permute-start(bf16[32,3072]{1,0:T(8,128)(2,1)S(1)} %slice_bitcast_fusion.6), channel_id=1, source_target_pairs={{0,8},{8,0},{16,24},{24,16},{1,9},{9,1},{17,25},{25,17},{2,10},{10... | collective-permute-start | bytes 589832 | tf_op jit(solution)/shard_map/ppermute | solution.py:331
  133.6 1.0 copy-start.1
